TPU v7x, 256 devices: a whole 4x4x8 slice. The times are simulated.
256 devices in a mesh: cell: 32 (over z, y_hi, core), period: 8 (over x, y_lo).
Axes of the slice: x: 4, y: 4 (y_hi: 2, y_lo: 2; y = y_hi * 2 + y_lo), z: 8, core: 2. Of those that a mesh axis runs over, the one named last changes fastest.
Arguments:
- footprints: float32 [32, 16, 32768], P(None, 'period', 'cell'), may hold values from -16 to 16
- cell_coords: int32 [2, 32768], P(None, 'cell'), may hold values from 0 to 255, as said below
- obs_period: int32 [32], replicated, may hold values from 0 to 15
- temporal_cov: float32 [16, 16], replicated, may hold values from -1.5 to 1.5
Outputs:
- hq_field: float32 [32, 16, 32768], P(None, 'period', 'cell')
- hqh_gram: float32 [32, 32], replicated
Inputs may be any that keep to these rules, and one draw needn't show every extreme that they name: `cell_coords`: cells sit at distinct grid points that together fill the rectangle of first coordinates 0 to 255 and second coordinates 0 to 127.
All inputs are finite; a program needn't handle non-finite values.
Results may differ from a plain program's by a relative error of at most 0.0003.
Values sent between devices are 32-bit elements; how exact they have to be, the bound alone decides.
No kernel may reach another device: no remote copies, remote signals or barrier semaphores. Data moves between devices by JAX's collectives and lax.ppermute only.
A program may use at most 64 MiB of HBM per device.

v0:
```python
import jax
import jax.numpy as jnp
from jax import lax
from jax.sharding import PartitionSpec as P

LENGTH_SCALE = 48.0
BLOCK_LIMIT = 4096


def covariance_tile(first_xy, second_xy):
    delta_x = first_xy[0][:, None] - second_xy[0][None, :]
    delta_y = first_xy[1][:, None] - second_xy[1][None, :]
    return jnp.exp(-jnp.sqrt(delta_x * delta_x + delta_y * delta_y) / LENGTH_SCALE)


def block_size(total_width, unit_width):
    unit_count = total_width // unit_width
    best_count = 1
    for factor in range(1, unit_count + 1):
        if unit_count % factor == 0 and factor * unit_width <= max(BLOCK_LIMIT, unit_width):
            best_count = factor
    return best_count * unit_width


def on_device(footprints, cell_coords, obs_period, temporal_cov):
    obs_count, per_local, cell_local = footprints.shape
    flat_count = obs_count * per_local
    period_first = lax.axis_index("period") * per_local
    period_ids = period_first + jnp.arange(per_local, dtype=jnp.int32)
    keep = (period_ids[None, :, None] <= obs_period[:, None, None]).astype(jnp.float32)
    masked = footprints * keep
    flat_rows = masked.reshape(flat_count, cell_local)
    local_places = cell_coords.astype(jnp.float32)
    empty = jnp.zeros((flat_count, cell_local), jnp.float32)
    piece_rows = lax.all_gather(flat_rows, "cell", axis=1, tiled=True)
    piece_places = lax.all_gather(local_places, "cell", axis=1, tiled=True)
    piece_width = piece_rows.shape[1]
    block_width = block_size(piece_width, cell_local)

    def add_block(block_index, running_sum):
        offset = block_index * block_width
        part_rows = lax.dynamic_slice_in_dim(piece_rows, offset, block_width, 1)
        part_places = lax.dynamic_slice_in_dim(piece_places, offset, block_width, 1)
        tile = covariance_tile(part_places, local_places)
        return running_sum + jnp.dot(
            part_rows, tile, precision=lax.Precision.HIGHEST, preferred_element_type=jnp.float32
        )

    spatial_flat = lax.fori_loop(0, piece_width // block_width, add_block, empty)
    spatial = spatial_flat.reshape(obs_count, per_local, cell_local)
    piece = lax.all_gather(spatial, "period", axis=1, tiled=True)
    weights = lax.dynamic_slice(temporal_cov, (period_first, 0), (per_local, piece.shape[1]))
    hq_field = jnp.einsum("tu,nuj->ntj", weights, piece, precision=lax.Precision.HIGHEST)
    partial_gram = jnp.einsum("ntj,mtj->nm", hq_field, masked, precision=lax.Precision.HIGHEST)
    hqh_gram = lax.psum(partial_gram, ("cell", "period"))
    return (hq_field, hqh_gram)


def solution(mesh):
    return jax.shard_map(
        on_device,
        mesh=mesh,
        in_specs=(P(None, "period", "cell"), P(None, "cell"), P(), P()),
        out_specs=(P(None, "period", "cell"), P()),
        check_vma=False,
    )
```

profile of v0, /device:TPU:1, one launch (start us, length us, event | category | flops | bytes accessed | tf_op | source)
XLA Modules:
  0.0 412.7 jit_solution(13719887616135554057)
XLA Ops:
  7.2 0.0 all-gather.3.cloned.1.call-start
  7.2 0.7 compare_convert_fusion
  8.0 0.1 copy.15
  8.1 1.1 broadcast_multiply_fusion
  9.2 0.9 reshape.51
  10.1 0.0 all-gather.5.cloned.1.call-start
  10.1 0.7 convert_element_type.12
  10.8 47.3 %all_gather.10 = f32[2,32768]{1,0:T(2,128)S(1)} all-gather(f32[2,1024]{1,0:T(2,128)S(1)} %convert_element_type.12), channel_id=1, replica_groups=mesh['cell'=32,'period'=8] {'cell'}, dimensions={1}, use_global_device_ids=true | all-gather | bytes 270336 | tf_op jit(solution)/shard_map/all_gather | solution.py:36
  58.1 58.6 %all-gather.3.cloned.1.call-done = f32[64,32768]{1,0:T(8,128)} async-done(((f32[64,1024]{1,0:T(8,128)}), f32[64,32768]{1,0:T(8,128)}) %all-gather.3.cloned.1.call-update) | async-done | bytes 8388624 | tf_op jit(solution)/shard_map/all_gather | solution.py:35
  116.7 157.3 %while.14 = (s32[]{:T(128)}, f32[64,1024]{1,0:T(8,128)S(1)}, f32[64,32768]{1,0:T(8,128)}, f32[2,32768]{1,0:T(2,128)S(1)}, f32[2,1024]{1,0:T(2,128)S(1)}, /*index...) while((s32[]{:T(128)}, f32[64,1024]{1,0:T(8,128)S(1)}, f32[64,32768]{1,0:T(8,128)}, ...), condition=%wide.region_1.0_spmd.clone, body=%wide.region_0.0_spmd.clone.sunk | while | flops 3250716672 | bytes 1695933 | solution.py:49
  116.7 0.1 constant_dynamic-slice_fusion.2
  116.8 19.5 %fusion.39 = f32[64,1024]{1,0:T(8,128)S(1)} fusion(f32[1024]{0:T(1024)S(1)} %bitcast.22, f32[4096]{0:T(1024)S(1)} %bitcast.20, f32[1024]{0:T(1024)S(1)} %bitcast.21, f32[4096]{0:T(1024)S(1)} %bitcast.19, f32[64,32768]{1,0:T(8,128)} %get-tuple-element.190, s32[]{:T(128)S(6)} %select_n.14, f32[64,1024]{1,0:T(8,128)S(1)} %get-tuple-element.179, ...), kind=kOutput, calls=%fused_computation.15.clone.1 | convolution fusion | flops 3250716672 | bytes 1613829 | tf_op jit(solution)/shard_map/while/body/eval_jaxpr/dot_general | solution.py:45
  136.3 0.1 constant_dynamic-slice_fusion.2
  136.4 19.5 %fusion.39 = f32[64,1024]{1,0:T(8,128)S(1)} fusion(f32[1024]{0:T(1024)S(1)} %bitcast.22, f32[4096]{0:T(1024)S(1)} %bitcast.20, f32[1024]{0:T(1024)S(1)} %bitcast.21, f32[4096]{0:T(1024)S(1)} %bitcast.19, f32[64,32768]{1,0:T(8,128)} %get-tuple-element.190, s32[]{:T(128)S(6)} %select_n.14, f32[64,1024]{1,0:T(8,128)S(1)} %get-tuple-element.179, ...), kind=kOutput, calls=%fused_computation.15.clone.1 | convolution fusion | flops 3250716672 | bytes 1613829 | tf_op jit(solution)/shard_map/while/body/eval_jaxpr/dot_general | solution.py:45
  156.0 0.1 constant_dynamic-slice_fusion.2
  156.1 19.5 %fusion.39 = f32[64,1024]{1,0:T(8,128)S(1)} fusion(f32[1024]{0:T(1024)S(1)} %bitcast.22, f32[4096]{0:T(1024)S(1)} %bitcast.20, f32[1024]{0:T(1024)S(1)} %bitcast.21, f32[4096]{0:T(1024)S(1)} %bitcast.19, f32[64,32768]{1,0:T(8,128)} %get-tuple-element.190, s32[]{:T(128)S(6)} %select_n.14, f32[64,1024]{1,0:T(8,128)S(1)} %get-tuple-element.179, ...), kind=kOutput, calls=%fused_computation.15.clone.1 | convolution fusion | flops 3250716672 | bytes 1613829 | tf_op jit(solution)/shard_map/while/body/eval_jaxpr/dot_general | solution.py:45
  175.6 0.1 constant_dynamic-slice_fusion.2
  175.7 19.5 %fusion.39 = f32[64,1024]{1,0:T(8,128)S(1)} fusion(f32[1024]{0:T(1024)S(1)} %bitcast.22, f32[4096]{0:T(1024)S(1)} %bitcast.20, f32[1024]{0:T(1024)S(1)} %bitcast.21, f32[4096]{0:T(1024)S(1)} %bitcast.19, f32[64,32768]{1,0:T(8,128)} %get-tuple-element.190, s32[]{:T(128)S(6)} %select_n.14, f32[64,1024]{1,0:T(8,128)S(1)} %get-tuple-element.179, ...), kind=kOutput, calls=%fused_computation.15.clone.1 | convolution fusion | flops 3250716672 | bytes 1613829 | tf_op jit(solution)/shard_map/while/body/eval_jaxpr/dot_general | solution.py:45
  195.3 0.1 constant_dynamic-slice_fusion.2
  195.4 19.5 %fusion.39 = f32[64,1024]{1,0:T(8,128)S(1)} fusion(f32[1024]{0:T(1024)S(1)} %bitcast.22, f32[4096]{0:T(1024)S(1)} %bitcast.20, f32[1024]{0:T(1024)S(1)} %bitcast.21, f32[4096]{0:T(1024)S(1)} %bitcast.19, f32[64,32768]{1,0:T(8,128)} %get-tuple-element.190, s32[]{:T(128)S(6)} %select_n.14, f32[64,1024]{1,0:T(8,128)S(1)} %get-tuple-element.179, ...), kind=kOutput, calls=%fused_computation.15.clone.1 | convolution fusion | flops 3250716672 | bytes 1613829 | tf_op jit(solution)/shard_map/while/body/eval_jaxpr/dot_general | solution.py:45
  214.9 0.1 constant_dynamic-slice_fusion.2
  215.0 19.5 %fusion.39 = f32[64,1024]{1,0:T(8,128)S(1)} fusion(f32[1024]{0:T(1024)S(1)} %bitcast.22, f32[4096]{0:T(1024)S(1)} %bitcast.20, f32[1024]{0:T(1024)S(1)} %bitcast.21, f32[4096]{0:T(1024)S(1)} %bitcast.19, f32[64,32768]{1,0:T(8,128)} %get-tuple-element.190, s32[]{:T(128)S(6)} %select_n.14, f32[64,1024]{1,0:T(8,128)S(1)} %get-tuple-element.179, ...), kind=kOutput, calls=%fused_computation.15.clone.1 | convolution fusion | flops 3250716672 | bytes 1613829 | tf_op jit(solution)/shard_map/while/body/eval_jaxpr/dot_general | solution.py:45
  234.6 0.1 constant_dynamic-slice_fusion.2
  234.7 19.5 %fusion.39 = f32[64,1024]{1,0:T(8,128)S(1)} fusion(f32[1024]{0:T(1024)S(1)} %bitcast.22, f32[4096]{0:T(1024)S(1)} %bitcast.20, f32[1024]{0:T(1024)S(1)} %bitcast.21, f32[4096]{0:T(1024)S(1)} %bitcast.19, f32[64,32768]{1,0:T(8,128)} %get-tuple-element.190, s32[]{:T(128)S(6)} %select_n.14, f32[64,1024]{1,0:T(8,128)S(1)} %get-tuple-element.179, ...), kind=kOutput, calls=%fused_computation.15.clone.1 | convolution fusion | flops 3250716672 | bytes 1613829 | tf_op jit(solution)/shard_map/while/body/eval_jaxpr/dot_general | solution.py:45
  254.2 0.1 constant_dynamic-slice_fusion.2
  254.3 19.5 %fusion.39 = f32[64,1024]{1,0:T(8,128)S(1)} fusion(f32[1024]{0:T(1024)S(1)} %bitcast.22, f32[4096]{0:T(1024)S(1)} %bitcast.20, f32[1024]{0:T(1024)S(1)} %bitcast.21, f32[4096]{0:T(1024)S(1)} %bitcast.19, f32[64,32768]{1,0:T(8,128)} %get-tuple-element.190, s32[]{:T(128)S(6)} %select_n.14, f32[64,1024]{1,0:T(8,128)S(1)} %get-tuple-element.179, ...), kind=kOutput, calls=%fused_computation.15.clone.1 | convolution fusion | flops 3250716672 | bytes 1613829 | tf_op jit(solution)/shard_map/while/body/eval_jaxpr/dot_general | solution.py:45
  274.0 0.1 reshape.52
  274.2 0.8 copy.16
  275.0 48.4 %all-gather.5.cloned.1.call-done = f32[32,16,1024]{2,0,1:T(8,128)} async-done(((f32[32,2,1024]{2,0,1:T(8,128)}), f32[32,16,1024]{2,0,1:T(8,128)}) %all-gather.5.cloned.1.call-update) | async-done | bytes 2097168 | tf_op jit(solution)/shard_map/all_gather | solution.py:51
  323.4 3.9 fusion.23
  327.3 0.5 convolution_bitcast_fusion
  327.7 78.1 %psum.7 = f32[32,32]{1,0:T(8,128)} all-reduce(f32[32,32]{1,0:T(8,128)S(1)} %convolution_bitcast_fusion), channel_id=1, replica_groups=mesh['cell'=32,'period'=8] {'cell','period'}, use_global_device_ids=true, to_apply=%region_2.0 | all-reduce | flops 1024 | bytes 8192 | tf_op jit(solution)/shard_map/psum | solution.py:55
  (16 shorter events, 0.1 us)
Async XLA Ops:
  7.2 316.2 %copy-start = (f32[16,16]{1,0:T(8,128)S(1)}, f32[16,16]{1,0:T(8,128)}, u32[]{:S(2)}) copy-start(f32[16,16]{1,0:T(8,128)} %param.9) | copy-start | bytes 3076
  7.2 109.5 %all-gather.3.cloned.1.call-start = ((), (), s32[]{:S(2)}) async-start(), calls=%async_computation | async-start | bytes 8650752 | tf_op jit(solution)/shard_map/all_gather | solution.py:35
  10.1 313.3 %all-gather.5.cloned.1.call-start = ((), (), s32[]{:S(2)}) async-start(), calls=%async_computation.1 | async-start | bytes 2359296 | tf_op jit(solution)/shard_map/all_gather | solution.py:51
  327.3 78.6 %copy-start.1 = (f32[32,2,1024]{2,1,0:T(2,128)}, f32[32,2,1024]{2,1,0:T(2,128)S(1)}, u32[]{:S(2)}) copy-start(f32[32,2,1024]{2,1,0:T(2,128)S(1)} %fusion.23) | copy-start | bytes 786436
Sparse Core Ops, SparseCore 0:
  11.4 105.2 all-gather.2
  275.1 48.2 all-gather.4
where the time goes:
time: 413 us
  matrix products  160 us (39%)
  blocking collectives  125 us (30%)
  waiting for transfers between devices  107 us (26%)
  between operations  14.1 us (3%)
    dot_general x8, matrix products, add_block(): jnp.dot(part_rows, tile, precision=lax.Precision.HIGHEST, preferred_eleme...  156 us
    psum x1, blocking collectives, on_device(): hqh_gram = lax.psum(partial_gram, ('cell', 'period'))  78.1 us
    all_gather x1, waiting for transfers between devices, on_device(): piece_rows = lax.all_gather(flat_rows, 'cell', axis=1, tiled=True)  58.6 us
    all_gather x1, waiting for transfers between devices, on_device(): piece = lax.all_gather(spatial, 'period', axis=1, tiled=True)  48.4 us
    all_gather x1, blocking collectives, on_device(): piece_places = lax.all_gather(local_places, 'cell', axis=1, tiled=True)  47.3 us
  transfers between devices with their start and end apart: 2, of which 2 were waited for; matrix products, arithmetic and copies ran while one was open for 0% of the time, Pallas kernels for 0%

commit v1 on v0

--- a/solution.py
+++ b/solution.py
@@ -52,7 +52,7 @@
     weights = lax.dynamic_slice(temporal_cov, (period_first, 0), (per_local, piece.shape[1]))
     hq_field = jnp.einsum("tu,nuj->ntj", weights, piece, precision=lax.Precision.HIGHEST)
     partial_gram = jnp.einsum("ntj,mtj->nm", hq_field, masked, precision=lax.Precision.HIGHEST)
-    hqh_gram = lax.psum(partial_gram, ("cell", "period"))
+    hqh_gram = jnp.sum(lax.all_gather(partial_gram, ("cell", "period")), axis=0)
     return (hq_field, hqh_gram)
 
 

time: 413 us -> 1060 us (2.57)
  waiting for transfers between devices: 107 us -> 827 us
  blocking collectives: 125 us -> 47.3 us
    all_gather x0 -> x1, waiting for transfers between devices: none -> 720 us  [on_device(): hqh_gram = jnp.sum(lax.all_gather(partial_gram, ('cell', 'period')), axis=0)]
    psum x1 -> x0, blocking collectives: 78.1 us -> none  [on_device(): hqh_gram = lax.psum(partial_gram, ('cell', 'period'))]
  transfers between devices with their start and end apart: 2 -> 3, of which waited for: 2 -> 3; matrix products, arithmetic and copies ran while one was open for 0% -> 0% of each run, Pallas kernels for 0% -> 0%
where the time goes in v1:
time: 1060 us
  waiting for transfers between devices  827 us (78%)
  matrix products  161 us (15%)
  blocking collectives  47.3 us (4%)
  between operations  13.8 us (1%)
    all_gather x1, waiting for transfers between devices, on_device(): hqh_gram = jnp.sum(lax.all_gather(partial_gram, ('cell', 'period')), axis=0)  720 us
    dot_general x8, matrix products, add_block(): jnp.dot(part_rows, tile, precision=lax.Precision.HIGHEST, preferred_eleme...  156 us
    all_gather x1, waiting for transfers between devices, on_device(): piece_rows = lax.all_gather(flat_rows, 'cell', axis=1, tiled=True)  58.6 us
    all_gather x1, waiting for transfers between devices, on_device(): piece = lax.all_gather(spatial, 'period', axis=1, tiled=True)  48.3 us
    all_gather x1, blocking collectives, on_device(): piece_places = lax.all_gather(local_places, 'cell', axis=1, tiled=True)  47.3 us
  transfers between devices with their start and end apart: 3, of which 3 were waited for; matrix products, arithmetic and copies ran while one was open for 0% of the time, Pallas kernels for 0%

profile of v1, /device:TPU:1, one launch (start us, length us, event | category | flops | bytes accessed | tf_op | source)
XLA Modules:
  0.0 1057.8 jit_solution(2075133454489124433)
XLA Ops:
  7.2 0.7 compare_convert_fusion
  8.0 0.1 copy.15
  8.1 1.1 broadcast_multiply_fusion
  9.2 0.9 reshape.51
  10.1 0.7 convert_element_type.12
  10.8 47.3 %all_gather.16 = f32[2,32768]{1,0:T(2,128)S(1)} all-gather(f32[2,1024]{1,0:T(2,128)S(1)} %convert_element_type.12), channel_id=1, replica_groups=mesh['cell'=32,'period'=8] {'cell'}, dimensions={1}, use_global_device_ids=true | all-gather | bytes 270336 | tf_op jit(solution)/shard_map/all_gather | solution.py:36
  58.1 58.6 %all-gather.5.cloned.1.call-done = f32[64,32768]{1,0:T(8,128)} async-done(((f32[64,1024]{1,0:T(8,128)}), f32[64,32768]{1,0:T(8,128)}) %all-gather.5.cloned.1.call-update) | async-done | bytes 8388624 | tf_op jit(solution)/shard_map/all_gather | solution.py:35
  116.7 157.3 %while.14 = (s32[]{:T(128)}, f32[64,1024]{1,0:T(8,128)S(1)}, f32[64,32768]{1,0:T(8,128)}, f32[2,32768]{1,0:T(2,128)S(1)}, f32[2,1024]{1,0:T(2,128)S(1)}, /*index...) while((s32[]{:T(128)}, f32[64,1024]{1,0:T(8,128)S(1)}, f32[64,32768]{1,0:T(8,128)}, ...), condition=%wide.region_1.0_spmd.clone, body=%wide.region_0.0_spmd.clone.sunk | while | flops 3250716672 | bytes 1695933 | solution.py:49
  116.7 0.1 constant_dynamic-slice_fusion.2
  116.8 19.5 %fusion.39 = f32[64,1024]{1,0:T(8,128)S(1)} fusion(f32[1024]{0:T(1024)S(1)} %bitcast.24, f32[4096]{0:T(1024)S(1)} %bitcast.22, f32[1024]{0:T(1024)S(1)} %bitcast.23, f32[4096]{0:T(1024)S(1)} %bitcast.21, f32[64,32768]{1,0:T(8,128)} %get-tuple-element.190, s32[]{:T(128)S(6)} %select_n.14, f32[64,1024]{1,0:T(8,128)S(1)} %get-tuple-element.179, ...), kind=kOutput, calls=%fused_computation.15.clone.1 | convolution fusion | flops 3250716672 | bytes 1613829 | tf_op jit(solution)/shard_map/while/body/eval_jaxpr/dot_general | solution.py:45
  136.3 0.1 constant_dynamic-slice_fusion.2
  136.4 19.5 %fusion.39 = f32[64,1024]{1,0:T(8,128)S(1)} fusion(f32[1024]{0:T(1024)S(1)} %bitcast.24, f32[4096]{0:T(1024)S(1)} %bitcast.22, f32[1024]{0:T(1024)S(1)} %bitcast.23, f32[4096]{0:T(1024)S(1)} %bitcast.21, f32[64,32768]{1,0:T(8,128)} %get-tuple-element.190, s32[]{:T(128)S(6)} %select_n.14, f32[64,1024]{1,0:T(8,128)S(1)} %get-tuple-element.179, ...), kind=kOutput, calls=%fused_computation.15.clone.1 | convolution fusion | flops 3250716672 | bytes 1613829 | tf_op jit(solution)/shard_map/while/body/eval_jaxpr/dot_general | solution.py:45
  156.0 0.1 constant_dynamic-slice_fusion.2
  156.1 19.5 %fusion.39 = f32[64,1024]{1,0:T(8,128)S(1)} fusion(f32[1024]{0:T(1024)S(1)} %bitcast.24, f32[4096]{0:T(1024)S(1)} %bitcast.22, f32[1024]{0:T(1024)S(1)} %bitcast.23, f32[4096]{0:T(1024)S(1)} %bitcast.21, f32[64,32768]{1,0:T(8,128)} %get-tuple-element.190, s32[]{:T(128)S(6)} %select_n.14, f32[64,1024]{1,0:T(8,128)S(1)} %get-tuple-element.179, ...), kind=kOutput, calls=%fused_computation.15.clone.1 | convolution fusion | flops 3250716672 | bytes 1613829 | tf_op jit(solution)/shard_map/while/body/eval_jaxpr/dot_general | solution.py:45
  175.6 0.1 constant_dynamic-slice_fusion.2
  175.7 19.5 %fusion.39 = f32[64,1024]{1,0:T(8,128)S(1)} fusion(f32[1024]{0:T(1024)S(1)} %bitcast.24, f32[4096]{0:T(1024)S(1)} %bitcast.22, f32[1024]{0:T(1024)S(1)} %bitcast.23, f32[4096]{0:T(1024)S(1)} %bitcast.21, f32[64,32768]{1,0:T(8,128)} %get-tuple-element.190, s32[]{:T(128)S(6)} %select_n.14, f32[64,1024]{1,0:T(8,128)S(1)} %get-tuple-element.179, ...), kind=kOutput, calls=%fused_computation.15.clone.1 | convolution fusion | flops 3250716672 | bytes 1613829 | tf_op jit(solution)/shard_map/while/body/eval_jaxpr/dot_general | solution.py:45
  195.3 0.1 constant_dynamic-slice_fusion.2
  195.4 19.5 %fusion.39 = f32[64,1024]{1,0:T(8,128)S(1)} fusion(f32[1024]{0:T(1024)S(1)} %bitcast.24, f32[4096]{0:T(1024)S(1)} %bitcast.22, f32[1024]{0:T(1024)S(1)} %bitcast.23, f32[4096]{0:T(1024)S(1)} %bitcast.21, f32[64,32768]{1,0:T(8,128)} %get-tuple-element.190, s32[]{:T(128)S(6)} %select_n.14, f32[64,1024]{1,0:T(8,128)S(1)} %get-tuple-element.179, ...), kind=kOutput, calls=%fused_computation.15.clone.1 | convolution fusion | flops 3250716672 | bytes 1613829 | tf_op jit(solution)/shard_map/while/body/eval_jaxpr/dot_general | solution.py:45
  214.9 0.1 constant_dynamic-slice_fusion.2
  215.0 19.5 %fusion.39 = f32[64,1024]{1,0:T(8,128)S(1)} fusion(f32[1024]{0:T(1024)S(1)} %bitcast.24, f32[4096]{0:T(1024)S(1)} %bitcast.22, f32[1024]{0:T(1024)S(1)} %bitcast.23, f32[4096]{0:T(1024)S(1)} %bitcast.21, f32[64,32768]{1,0:T(8,128)} %get-tuple-element.190, s32[]{:T(128)S(6)} %select_n.14, f32[64,1024]{1,0:T(8,128)S(1)} %get-tuple-element.179, ...), kind=kOutput, calls=%fused_computation.15.clone.1 | convolution fusion | flops 3250716672 | bytes 1613829 | tf_op jit(solution)/shard_map/while/body/eval_jaxpr/dot_general | solution.py:45
  234.6 0.1 constant_dynamic-slice_fusion.2
  234.7 19.5 %fusion.39 = f32[64,1024]{1,0:T(8,128)S(1)} fusion(f32[1024]{0:T(1024)S(1)} %bitcast.24, f32[4096]{0:T(1024)S(1)} %bitcast.22, f32[1024]{0:T(1024)S(1)} %bitcast.23, f32[4096]{0:T(1024)S(1)} %bitcast.21, f32[64,32768]{1,0:T(8,128)} %get-tuple-element.190, s32[]{:T(128)S(6)} %select_n.14, f32[64,1024]{1,0:T(8,128)S(1)} %get-tuple-element.179, ...), kind=kOutput, calls=%fused_computation.15.clone.1 | convolution fusion | flops 3250716672 | bytes 1613829 | tf_op jit(solution)/shard_map/while/body/eval_jaxpr/dot_general | solution.py:45
  254.2 0.1 constant_dynamic-slice_fusion.2
  254.3 19.5 %fusion.39 = f32[64,1024]{1,0:T(8,128)S(1)} fusion(f32[1024]{0:T(1024)S(1)} %bitcast.24, f32[4096]{0:T(1024)S(1)} %bitcast.22, f32[1024]{0:T(1024)S(1)} %bitcast.23, f32[4096]{0:T(1024)S(1)} %bitcast.21, f32[64,32768]{1,0:T(8,128)} %get-tuple-element.190, s32[]{:T(128)S(6)} %select_n.14, f32[64,1024]{1,0:T(8,128)S(1)} %get-tuple-element.179, ...), kind=kOutput, calls=%fused_computation.15.clone.1 | convolution fusion | flops 3250716672 | bytes 1613829 | tf_op jit(solution)/shard_map/while/body/eval_jaxpr/dot_general | solution.py:45
  274.0 0.1 reshape.52
  274.2 0.8 copy.16
  275.0 0.0 all-gather.9.cloned.1.call-start
  275.1 48.3 %all-gather.7.cloned.1.call-done = f32[32,16,1024]{2,0,1:T(8,128)} async-done(((f32[32,2,1024]{2,0,1:T(8,128)}), f32[32,16,1024]{2,0,1:T(8,128)}) %all-gather.7.cloned.1.call-update) | async-done | bytes 2097168 | tf_op jit(solution)/shard_map/all_gather | solution.py:51
  323.4 3.9 fusion.23
  327.3 1.1 convolution_bitcast_fusion
  328.4 719.7 %all-gather.9.cloned.1.call-done = f32[8192,32]{1,0:T(8,128)} async-done(((f32[32,32]{1,0:T(8,128)}), f32[8192,32]{1,0:T(8,128)}) %all-gather.9.cloned.1.call-update) | async-done | bytes 1048592 | tf_op jit(solution)/shard_map/all_gather | solution.py:55
  1048.1 3.1 reduce_sum.9
  (19 shorter events, 0.2 us)
Async XLA Ops:
  7.2 316.2 %copy-start = (f32[16,16]{1,0:T(8,128)S(1)}, f32[16,16]{1,0:T(8,128)}, u32[]{:S(2)}) copy-start(f32[16,16]{1,0:T(8,128)} %param.9) | copy-start | bytes 3076
  7.2 109.5 %all-gather.5.cloned.1.call-start = ((), (), s32[]{:S(2)}) async-start(), calls=%async_computation | async-start | bytes 8650752 | tf_op jit(solution)/shard_map/all_gather | solution.py:35
  10.1 313.3 %all-gather.7.cloned.1.call-start = ((), (), s32[]{:S(2)}) async-start(), calls=%async_computation.1 | async-start | bytes 2359296 | tf_op jit(solution)/shard_map/all_gather | solution.py:51
  275.0 773.1 %all-gather.9.cloned.1.call-start = ((), (), s32[]{:S(2)}) async-start(), calls=%async_computation.2 | async-start | bytes 4210688 | tf_op jit(solution)/shard_map/all_gather | solution.py:55
  327.3 724.0 %copy-start.1 = (f32[32,2,1024]{2,1,0:T(2,128)}, f32[32,2,1024]{2,1,0:T(2,128)S(1)}, u32[]{:S(2)}) copy-start(f32[32,2,1024]{2,1,0:T(2,128)S(1)} %fusion.23) | copy-start | bytes 786436
Sparse Core Ops, SparseCore 0:
  11.4 105.2 all-gather.4
  275.1 48.2 all-gather.6
  328.5 719.5 all-gather.8
